TPU v7x, 512 devices: a whole 4x4x16 slice. The times are simulated.
512 devices in a mesh: ex: 64 (over y_lo, z, core), hid: 8 (over x, y_hi).
Axes of the slice: x: 4, y: 4 (y_hi: 2, y_lo: 2; y = y_hi * 2 + y_lo), z: 16, core: 2. Of those that a mesh axis runs over, the one named last changes fastest.
Arguments:
- activations: bfloat16 [256, 192, 14336], P('ex', None, 'hid'), may hold values from -6 to 6
- out_grads: bfloat16 [256, 192, 4096], P('ex', None, 'hid'), may hold values from -6 to 6
- token_mask: int32 [256, 192], P('ex'), may hold values from 0 to 1, as said below
- proj_in: bfloat16 [14336, 64], P('hid'), may hold values from -0.046875 to 0.046875
- proj_out: bfloat16 [4096, 64], P('hid'), may hold values from -0.09375 to 0.09375
- inv_input: float32 [64, 64], replicated, as said below
- inv_output: float32 [64, 64], replicated, as said below
- query_feats: bfloat16 [4096, 4096], P('ex', 'hid'), may hold values from -6 to 6
Outputs:
- scores: float32 [4096, 256], P('ex', 'hid')
Inputs may be any that keep to these rules, and one draw needn't show every extreme that they name: `token_mask`: each row is 48 or more ones followed by zeros; some row is all ones. `inv_input`: symmetric. `inv_output`: symmetric.
All inputs are finite; a program needn't handle non-finite values.
Results may differ from a plain program's by a relative error of at most 0.0041.
Values may be sent and summed in bfloat16 or wider, within the bound.
A program may use at most 64 MiB of HBM per device.

v0:
```python
import jax
import jax.numpy as jnp
from jax import lax
from jax.sharding import PartitionSpec as P


def local(
    activations, out_grads, token_mask, proj_in, proj_out, inv_input, inv_output, query_feats
):
    seq_count, length, unit_local = activations.shape
    rank_width = proj_in.shape[1]
    hid_size = lax.axis_size("hid")
    row_block = rank_width // hid_size
    my_index = lax.axis_index("hid")
    in_part = jnp.dot(
        activations.reshape(seq_count * length, unit_local),
        proj_in,
        preferred_element_type=jnp.float32,
    )
    in_part = jnp.dot(in_part, inv_input, precision=lax.Precision.HIGHEST)
    out_part = jnp.dot(
        out_grads.reshape(seq_count * length, out_grads.shape[2]),
        proj_out,
        preferred_element_type=jnp.float32,
    )
    token_weight = token_mask.astype(jnp.float32)
    tok_count = jnp.sum(token_weight, axis=1)
    in_full, out_full = lax.psum((in_part, out_part), "hid")
    in_mine = lax.dynamic_slice_in_dim(in_full, my_index * row_block, row_block, 1)
    masked = in_mine.reshape(seq_count, length, row_block) * token_weight[:, :, None]
    outer = jnp.einsum(
        "slr,slq->srq",
        masked,
        out_full.reshape(seq_count, length, rank_width),
        precision=lax.Precision.HIGHEST,
    )
    train_feats = (
        (outer / tok_count[:, None, None])
        .astype(jnp.bfloat16)
        .reshape(seq_count, row_block * rank_width)
    )
    query_count = query_feats.shape[0]
    queries = query_feats.reshape(query_count, row_block, rank_width).astype(jnp.float32)
    query_pre = jnp.einsum("qij,jk->qik", queries, inv_output, precision=lax.Precision.HIGHEST)
    query_pre = query_pre.astype(jnp.bfloat16).reshape(query_count, row_block * rank_width)
    partial_value = jnp.einsum(
        "qk,tk->qt",
        query_pre,
        lax.all_gather(train_feats, "ex", axis=0, tiled=True),
        preferred_element_type=jnp.float32,
    )
    return lax.psum_scatter(partial_value, "hid", scatter_dimension=1, tiled=True)


def solution(mesh):
    return jax.shard_map(
        local,
        mesh=mesh,
        in_specs=(
            P("ex", None, "hid"),
            P("ex", None, "hid"),
            P("ex", None),
            P("hid", None),
            P("hid", None),
            P(),
            P(),
            P("ex", "hid"),
        ),
        out_specs=P("ex", "hid"),
        check_vma=False,
    )
```

profile of v0, /device:TPU:2, one launch (start us, length us, event | category | flops | bytes accessed | tf_op | source)
XLA Modules:
  0.0 264.8 jit_solution(6362297296101887833)
XLA Ops:
  6.5 1.6 fusion.6
  8.2 0.2 reshape.28
  8.4 0.0 copy-start.3
  8.4 0.7 copy.17
  9.2 1.9 fusion.4
  11.1 0.0 copy-done.3
  11.1 1.0 fusion.5
  12.2 0.0 all-reduce.3.cloned.1.call-update
  12.2 0.0 reduce-scatter.2.cloned.1.call-start
  12.3 0.1 reshape.23
  12.4 0.2 convolution_convert_fusion
  12.7 0.1 copy.16
  12.8 0.1 reshape.24
  12.9 0.1 convert_reduce_fusion
  13.0 103.1 %all-reduce.3.cloned.1.call-done = (f32[4,192,64]{1,2,0:T(8,128)}, f32[768,64]{0,1:T(8,128)}) async-done(((f32[4,192,64]{1,2,0:T(8,128)}, f32[768,64]{0,1:T(8,128)}), (f32[4,192,64]{1,2,0:T(8,128)}, f32[768,64]{0,1:T(8,128)})) %all-reduce.3.cloned.1.call-update) | async-done | bytes 393232 | tf_op jit(solution)/shard_map/psum | solution.py:28
  116.1 0.7 constant_dynamic-slice_fusion
  116.9 0.1 reshape.26
  117.0 1.3 fusion
  118.3 0.1 reshape.30
  118.3 64.0 %all-gather = bf16[64,4,512]{2,1,0:T(4,128)(2,1)S(1)} all-gather(bf16[1,4,512]{2,1,0:T(4,128)(2,1)S(1)} %reshape.30), channel_id=1, replica_groups=mesh['ex'=64,'hid'=8] {'ex'}, dimensions={0}, use_global_device_ids=true | all-gather | bytes 266240 | tf_op jit(solution)/shard_map/all_gather | solution.py:49
  182.3 0.1 reshape.31
  182.4 0.9 fusion.7
  183.3 0.0 reduce-scatter.2.cloned.1.call-update
  183.3 74.7 %reduce-scatter.2.cloned.1.call-done = f32[64,32]{0,1:T(8,128)} async-done(((f32[64,256]{0,1:T(8,128)}), f32[64,32]{0,1:T(8,128)}) %reduce-scatter.2.cloned.1.call-update) | async-done | bytes 8208 | tf_op jit(solution)/shard_map/reduce_scatter | solution.py:52
  (12 shorter events, 0.0 us)
Async XLA Ops:
  6.5 2.6 copy-start
  6.5 109.6 %all-reduce.3.cloned.1.call-start = ((), (), s32[]{:S(2)}) async-start(), calls=%async_computation.2 | async-start | bytes 917504 | tf_op jit(solution)/shard_map/psum | solution.py:28
  8.4 2.7 %copy-start.3 = (f32[64,64]{1,0:T(8,128)S(1)}, f32[64,64]{1,0:T(8,128)}, u32[]{:S(2)}) copy-start(f32[64,64]{1,0:T(8,128)} %param.13) | copy-start | bytes 49156
  9.2 3.1 %copy-start.4 = (s32[4,192]{1,0:T(4,128)S(1)}, s32[4,192]{1,0:T(4,128)}, u32[]{:S(2)}) copy-start(s32[4,192]{1,0:T(4,128)} %param.10) | copy-start | bytes 9220
  9.2 3.1 %copy-start.1 = (bf16[64,512]{1,0:T(8,128)(2,1)S(1)}, bf16[64,512]{1,0:T(8,128)(2,1)}, u32[]{:S(2)}) copy-start(bf16[64,512]{1,0:T(8,128)(2,1)} %param.15) | copy-start | bytes 196612
  9.2 3.2 %copy-start.2 = (f32[64,64]{1,0:T(8,128)S(1)}, f32[64,64]{1,0:T(8,128)}, u32[]{:S(2)}) copy-start(f32[64,64]{1,0:T(8,128)} %param.14) | copy-start | bytes 49156
  12.2 245.8 %reduce-scatter.2.cloned.1.call-start = ((), (), s32[]{:S(2)}) async-start(), calls=%async_computation.1 | async-start | bytes 147456 | tf_op jit(solution)/shard_map/reduce_scatter | solution.py:52
Sparse Core Ops, SparseCore 0:
  12.3 103.7 all-reduce.2
  183.4 74.5 reduce-scatter.1
where the time goes:
time: 265 us
  waiting for transfers between devices  178 us (67%)
  blocking collectives  64 us (24%)
  between operations  13.5 us (5%)
  matrix products  6.98 us (3%)
    psum x1, waiting for transfers between devices, local(): in_full, out_full = lax.psum((in_part, out_part), 'hid')  103 us
    reduce_scatter x1, waiting for transfers between devices, local(): lax.psum_scatter(partial_value, 'hid', scatter_dimension=1, tiled=True)  74.7 us
    all_gather x1, blocking collectives, local(): lax.all_gather(train_feats, 'ex', axis=0, tiled=True)  64 us
  transfers between devices with their start and end apart: 2, of which 2 were waited for; matrix products, arithmetic and copies ran while one was open for 0% of the time, Pallas kernels for 0%

commit v1 on v0

--- a/solution.py
+++ b/solution.py
@@ -46,7 +46,9 @@
     partial_value = jnp.einsum(
         "qk,tk->qt",
         query_pre,
-        lax.all_gather(train_feats, "ex", axis=0, tiled=True),
+        jnp.concatenate(
+            lax.all_to_all(jnp.stack([train_feats] * lax.axis_size("ex")), "ex", 0, 0), axis=0
+        ),
         preferred_element_type=jnp.float32,
     )
     return lax.psum_scatter(partial_value, "hid", scatter_dimension=1, tiled=True)

time: 265 us -> 239 us (0.902)
  blocking collectives: 64 us -> 0 us
  waiting for transfers between devices: 178 us -> 201 us
  starting transfers between devices: 0.04 us -> 13.3 us
    all_gather x1 -> x0, blocking collectives: 64 us -> none  [local(): lax.all_gather(train_feats, 'ex', axis=0, tiled=True)]
    all_to_all x0 -> x1, waiting for transfers between devices: none -> 20.7 us  [local(): lax.all_to_all(jnp.stack([train_feats] * lax.axis_size('ex')), 'ex', 0, 0)]
    all_to_all x0 -> x1, starting transfers between devices: none -> 13.2 us  [local(): lax.all_to_all(jnp.stack([train_feats] * lax.axis_size('ex')), 'ex', 0, 0)]
  transfers between devices with their start and end apart: 2 -> 3, of which waited for: 2 -> 3; matrix products, arithmetic and copies ran while one was open for 0% -> 0% of each run, Pallas kernels for 0% -> 0%
where the time goes in v1:
time: 239 us; the launch traced here: 238 us
  waiting for transfers between devices  201 us (84%)
  between operations  13.5 us (6%)
  starting transfers between devices  13.3 us (6%)
  matrix products  7.13 us (3%)
  local copies, waits for them, and re-layouts  3.11 us (1%)
    psum x1, waiting for transfers between devices, local(): in_full, out_full = lax.psum((in_part, out_part), 'hid')  104 us
    reduce_scatter x1, waiting for transfers between devices, local(): lax.psum_scatter(partial_value, 'hid', scatter_dimension=1, tiled=True)  76.8 us
    all_to_all x1, waiting for transfers between devices, local(): lax.all_to_all(jnp.stack([train_feats] * lax.axis_size('ex')), 'ex', 0, 0)  20.7 us
    all_to_all x1, starting transfers between devices, local(): lax.all_to_all(jnp.stack([train_feats] * lax.axis_size('ex')), 'ex', 0, 0)  13.2 us
  transfers between devices with their start and end apart: 3, of which 3 were waited for; matrix products, arithmetic and copies ran while one was open for 0% of the time, Pallas kernels for 0%

profile of v1, /device:TPU:2, one launch (start us, length us, event | category | flops | bytes accessed | tf_op | source)
XLA Modules:
  0.0 238.5 jit_solution(5738096975588881693)
XLA Ops:
  6.5 1.6 fusion.6
  8.2 0.2 reshape.30
  8.4 0.7 copy.13
  9.2 1.8 fusion.4
  11.0 1.3 fusion.5
  12.3 0.0 all-reduce.3.cloned.1.call-update
  12.3 0.1 convert_reduce_fusion
  12.5 103.8 %all-reduce.3.cloned.1.call-done = (f32[4,192,64]{1,2,0:T(8,128)}, f32[768,64]{0,1:T(8,128)}) async-done(((f32[4,192,64]{1,2,0:T(8,128)}, f32[768,64]{0,1:T(8,128)}), (f32[4,192,64]{1,2,0:T(8,128)}, f32[768,64]{0,1:T(8,128)})) %all-reduce.3.cloned.1.call-update) | async-done | bytes 393232 | tf_op jit(solution)/shard_map/psum | solution.py:28
  116.3 0.7 constant_dynamic-slice_fusion
  117.0 0.1 reshape.28
  117.2 1.3 fusion
  118.4 0.1 stack_reshape.2
  118.5 0.8 stack.3
  119.3 13.2 %all-to-all-start = ((bf16[64,4,512]{2,1,0:T(4,128)(2,1)}), bf16[64,4,512]{2,1,0:T(4,128)(2,1)S(1)}, u32[]{:S(2)}, u32[]{:S(2)}) async-start(bf16[64,4,512]{2,1,0:T(4,128)(2,1)} %stack.3), calls=%async_computation | async-start | bytes 524288 | tf_op jit(solution)/shard_map/all_to_all | solution.py:50
  132.5 0.0 reduce-scatter.2.cloned.1.call-start
  132.6 0.1 reshape.25
  132.7 0.2 convolution_convert_fusion
  133.0 0.1 copy.12
  133.1 0.1 reshape.26
  133.2 20.7 %all-to-all-done = bf16[64,4,512]{2,1,0:T(4,128)(2,1)S(1)} async-done(((bf16[64,4,512]{2,1,0:T(4,128)(2,1)}), bf16[64,4,512]{2,1,0:T(4,128)(2,1)S(1)}, u32[]{:S(2)}, u32[]{:S(2)}) %all-to-all-start) | async-done | bytes 262176 | tf_op jit(solution)/shard_map/all_to_all | solution.py:50
  153.9 0.1 reshape.31
  154.0 0.9 fusion.7
  154.8 0.0 reduce-scatter.2.cloned.1.call-update
  154.9 76.8 %reduce-scatter.2.cloned.1.call-done = f32[64,32]{0,1:T(8,128)} async-done(((f32[64,256]{0,1:T(8,128)}), f32[64,32]{0,1:T(8,128)}) %reduce-scatter.2.cloned.1.call-update) | async-done | bytes 8208 | tf_op jit(solution)/shard_map/reduce_scatter | solution.py:54
  (14 shorter events, 0.0 us)
Async XLA Ops:
  6.5 2.6 %copy-start = (bf16[4,192,1792]{2,1,0:T(8,128)(2,1)S(1)}, bf16[4,192,1792]{2,1,0:T(8,128)(2,1)}, u32[]{:S(2)}) copy-start(bf16[4,192,1792]{2,1,0:T(8,128)(2,1)} %param.8) | copy-start | bytes 8257540
  6.5 109.8 %all-reduce.3.cloned.1.call-start = ((), (), s32[]{:S(2)}) async-start(), calls=%async_computation.3 | async-start | bytes 917504 | tf_op jit(solution)/shard_map/psum | solution.py:28
  9.1 1.9 copy-start.2
  9.1 3.2 %copy-start.4 = (s32[4,192]{1,0:T(4,128)S(1)}, s32[4,192]{1,0:T(4,128)}, u32[]{:S(2)}) copy-start(s32[4,192]{1,0:T(4,128)} %param.10) | copy-start | bytes 9220
  9.1 123.4 %copy-start.1 = (bf16[64,512]{1,0:T(8,128)(2,1)S(1)}, bf16[64,512]{1,0:T(8,128)(2,1)}, u32[]{:S(2)}) copy-start(bf16[64,512]{1,0:T(8,128)(2,1)} %param.15) | copy-start | bytes 196612
  9.1 123.6 %copy-start.3 = (f32[64,64]{1,0:T(8,128)S(1)}, f32[64,64]{1,0:T(8,128)}, u32[]{:S(2)}) copy-start(f32[64,64]{1,0:T(8,128)} %param.14) | copy-start | bytes 49156
  119.3 34.6 %all-to-all-start = ((bf16[64,4,512]{2,1,0:T(4,128)(2,1)}), bf16[64,4,512]{2,1,0:T(4,128)(2,1)S(1)}, u32[]{:S(2)}, u32[]{:S(2)}) async-start(bf16[64,4,512]{2,1,0:T(4,128)(2,1)} %stack.3), calls=%async_computation | async-start | bytes 524288 | tf_op jit(solution)/shard_map/all_to_all | solution.py:50
  132.5 99.1 %reduce-scatter.2.cloned.1.call-start = ((), (), s32[]{:S(2)}) async-start(), calls=%async_computation.2 | async-start | bytes 147456 | tf_op jit(solution)/shard_map/reduce_scatter | solution.py:54
Sparse Core Ops, SparseCore 0:
  12.4 103.8 all-reduce.2
  155.0 76.6 reduce-scatter.1
